TPU v7x, 128 devices: a whole 4x4x4 slice. The times are simulated.
128 devices in a mesh: dom: 8 (over z, core), grp: 16 (over x, y).
Axes of the slice: x: 4, y: 4, z: 4, core: 2. Of those that a mesh axis runs over, the one named last changes fastest.
Arguments:
- src_table: float32 [16384, 400], P(('dom', 'grp')), may hold values from -8 to 8
- src_state: float32 [16384], P(('dom', 'grp')), may hold values from 0.01 to 1
- tgt_table: float32 [131072, 400], P(('dom', 'grp')), may hold values from -8 to 8
- tgt_state: float32 [131072], P(('dom', 'grp')), may hold values from 0.01 to 1
- pair_source: int32 [2, 131072], P(None, ('dom', 'grp')), may hold values from 0 to 127
- pair_owner: int32 [2, 131072, 1], P(None, ('dom', 'grp')), may hold values from 0 to 15; in each aligned block of 1024 rows (0 to 1023, 1024 to 2047, ..., all dimensions but the last counted through in order) at most 256 rows name the same one
- pair_offset: int32 [2, 131072], P(None, ('dom', 'grp')), may hold values from 0 to 1023
- negatives: int32 [8, 1000], P('dom'), may hold values from 0 to 16383
- plan: int32 [2, 8], replicated, may hold values from 0 to 7, each once within a row
Outputs:
- src_trained: float32 [16384, 400], P(('dom', 'grp'))
- src_accum: float32 [16384], P(('dom', 'grp'))
- tgt_trained: float32 [131072, 400], P(('dom', 'grp'))
- tgt_accum: float32 [131072], P(('dom', 'grp'))
Inputs may be any that keep to these rules, and one draw needn't show every extreme that they name: `pair_owner`: in every round the pairs of one device name each owner at most 256 times, and some device's pairs name some owner exactly 256 times. `plan`: each round's row names every dom index once.
All inputs are finite; a program needn't handle non-finite values.
Results may differ from a plain program's by a relative error of at most 0.011.
Values may be sent and summed in bfloat16 or wider, within the bound.
No kernel may reach another device: no remote copies, remote signals or barrier semaphores. Data moves between devices by JAX's collectives and lax.ppermute only.
A program may use at most 128 MiB of HBM per device.

v0:
```python
import jax
import jax.numpy as jnp
from jax import lax
from jax.sharding import PartitionSpec as P

LEARN = 0.1


def adagrad(emb_table, opt_state, grads):
    new_state = opt_state + jnp.mean(grads * grads, axis=1)
    return (emb_table - LEARN * grads / jnp.sqrt(new_state)[:, None], new_state)


def slot_holding(sched_row, wanted):
    return jnp.sum(
        jnp.arange(sched_row.shape[0], dtype=jnp.int32) * (sched_row == wanted).astype(jnp.int32)
    )


def relayout(emb_table, opt_state, want_slot):
    carried = (jnp.zeros_like(emb_table), jnp.zeros_like(opt_state))
    pieces = (
        lax.all_gather(emb_table, "dom", axis=0, tiled=True),
        lax.all_gather(opt_state, "dom", axis=0, tiled=True),
    )
    row_count = carried[0].shape[0]
    row_total = pieces[0].shape[0]
    local_index = jnp.arange(row_count, dtype=jnp.int32) + want_slot * row_count
    is_inside = (local_index >= 0) & (local_index < row_total)
    safe_index = jnp.clip(local_index, 0, row_total - 1)
    new_rows = jnp.where(is_inside[:, None], jnp.take(pieces[0], safe_index, axis=0), carried[0])
    new_state = jnp.where(is_inside, jnp.take(pieces[1], safe_index, axis=0), carried[1])
    return (new_rows, new_state)


def train_round(
    held_table, held_state, tgt_table, tgt_state, sources, owners, offsets, neg_ids, my_grp
):
    group_count = lax.axis_size("grp")
    src_count, emb_width = held_table.shape
    tgt_count = tgt_table.shape[0]
    pair_count = sources.shape[0]
    capacity = pair_count // 4
    slot_count = group_count * capacity
    owned_ids = neg_ids - my_grp * tgt_count
    is_mine = (owned_ids >= 0) & (owned_ids < tgt_count)
    owned_safe = jnp.clip(owned_ids, 0, tgt_count - 1)
    src_bf = held_table.astype(jnp.bfloat16)
    tgt_bf = tgt_table.astype(jnp.bfloat16)
    local_rows = jnp.where(is_mine[:, None], jnp.take(tgt_table, owned_safe, axis=0), 0.0)
    neg_rows = lax.psum(local_rows, "grp").astype(jnp.bfloat16)
    dest_onehot = (owners[:, None] == jnp.arange(group_count, dtype=jnp.int32)[None, :]).astype(
        jnp.int32
    )
    slot_rank = jnp.sum((jnp.cumsum(dest_onehot, axis=0) - 1) * dest_onehot, axis=1)
    slot_place = owners * capacity + slot_rank
    out_offsets = jnp.full((slot_count,), -1, jnp.int32).at[slot_place].set(offsets)
    outgoing = (
        jnp.zeros((slot_count, emb_width), jnp.bfloat16)
        .at[slot_place]
        .set(jnp.take(src_bf, sources, axis=0))
    )
    incoming, got_offsets = (
        lax.all_to_all(
            outgoing.reshape(group_count, capacity, emb_width),
            "grp",
            split_axis=0,
            concat_axis=0,
            tiled=True,
        ),
        lax.all_to_all(
            out_offsets.reshape(group_count, capacity),
            "grp",
            split_axis=0,
            concat_axis=0,
            tiled=True,
        ),
    )
    incoming = incoming.reshape(slot_count, emb_width)
    got_offsets = got_offsets.reshape(slot_count)
    is_valid = (got_offsets >= 0).astype(jnp.float32)
    safe_offsets = jnp.clip(got_offsets, 0, tgt_count - 1)
    target_rows = jnp.take(tgt_bf, safe_offsets, axis=0)
    positive = jnp.einsum("sd,sd->s", incoming, target_rows, preferred_element_type=jnp.float32)
    negative = lax.dot_general(
        incoming, neg_rows, (((1,), (1,)), ((), ())), preferred_element_type=jnp.float32
    )
    score_max = jnp.maximum(jnp.max(negative, axis=1), positive)
    pos_exp = jnp.exp(positive - score_max)
    neg_exp = jnp.exp(negative - score_max[:, None])
    exp_total = pos_exp + jnp.sum(neg_exp, axis=1)
    d_pos = (pos_exp / exp_total - 1.0) * is_valid
    d_neg = (neg_exp / exp_total[:, None] * is_valid[:, None]).astype(jnp.bfloat16)
    source_grad = (
        d_pos[:, None] * target_rows.astype(jnp.float32)
        + jnp.dot(d_neg, neg_rows, preferred_element_type=jnp.float32)
    ).astype(jnp.bfloat16)
    returned = lax.all_to_all(
        source_grad.reshape(group_count, capacity, emb_width),
        "grp",
        split_axis=0,
        concat_axis=0,
        tiled=True,
    ).reshape(slot_count, emb_width)
    pair_grad = jnp.take(returned, slot_place, axis=0).astype(jnp.float32)
    src_grads = jnp.zeros((src_count, emb_width), jnp.float32).at[sources].add(pair_grad)
    tgt_grads = (
        jnp.zeros((tgt_count, emb_width), jnp.float32)
        .at[safe_offsets]
        .add(d_pos[:, None] * incoming.astype(jnp.float32))
    )
    neg_part = lax.dot_general(
        d_neg, incoming, (((0,), (0,)), ((), ())), preferred_element_type=jnp.float32
    )
    summed = lax.psum(neg_part, "grp")
    tgt_grads = tgt_grads.at[owned_safe].add(jnp.where(is_mine[:, None], summed, 0.0))
    held_table, held_state = adagrad(held_table, held_state, src_grads)
    tgt_table, tgt_state = adagrad(tgt_table, tgt_state, tgt_grads)
    return (held_table, held_state, tgt_table, tgt_state)


def shards(
    src_table,
    src_state,
    tgt_table,
    tgt_state,
    pair_source,
    pair_owner,
    pair_offset,
    negatives,
    plan,
):
    my_dom = lax.axis_index("dom")
    my_grp = lax.axis_index("grp")
    round_count = plan.shape[0]
    neg_ids = negatives[0]
    for round_index in range(round_count):
        held_table, held_state = relayout(src_table, src_state, plan[round_index, my_dom])
        held_table, held_state, tgt_table, tgt_state = train_round(
            held_table,
            held_state,
            tgt_table,
            tgt_state,
            pair_source[round_index],
            pair_owner[round_index, :, 0],
            pair_offset[round_index],
            neg_ids,
            my_grp,
        )
        src_table, src_state = relayout(
            held_table, held_state, slot_holding(plan[round_index], my_dom)
        )
    return (src_table, src_state, tgt_table, tgt_state)


def solution(mesh):
    return jax.shard_map(
        shards,
        mesh=mesh,
        in_specs=(
            P(("dom", "grp"), None),
            P(("dom", "grp")),
            P(("dom", "grp"), None),
            P(("dom", "grp")),
            P(None, ("dom", "grp")),
            P(None, ("dom", "grp"), None),
            P(None, ("dom", "grp")),
            P("dom", None),
            P(),
        ),
        out_specs=(
            P(("dom", "grp"), None),
            P(("dom", "grp")),
            P(("dom", "grp"), None),
            P(("dom", "grp")),
        ),
        check_vma=False,
    )
```

profile of v0, /device:TPU:1, one launch (start us, length us, event | category | flops | bytes accessed | tf_op | source)
XLA Modules:
  0.0 816.0 jit_solution(2772978685348490794)
XLA Ops:
  9.7 4.5 reduce-window.16
  14.6 4.5 reduce-window.14
  22.4 4.9 scatter_custom_fusion
  27.2 7.6 all-to-all-start
  42.0 13.0 %scatter_custom_fusion.1 = bf16[4096,400]{1,0:T(8,128)(2,1)} fusion(s32[1024]{0:T(1024)S(1)} %bitcast.168, bf16[]{:T(256)} %constant.84.clone.1, pred[1024]{0:T(1024)(128)(4,1)S(1)} %compare_and_fusion.6, bf16[]{:T(256)} %constant.29.clone.2, bf16[128,400]{1,0:T(8,128)(2,1)S(1)} %fusion.38, s32[1024]{0:T(1024)S(1)} %fusion.56), kind=kCustom, calls=%fused_computation.58 | custom fusion | flops 409600 | bytes 3412996 | tf_op jit(solution)/shard_map/scatter | solution.py:61
  55.0 6.1 copy.80
  61.1 6.6 all-to-all-start.1
  72.5 4.9 gather_fusion.2
  83.4 97.5 %all-reduce.8 = bf16[1000,400]{0,1:T(8,128)(2,1)} all-reduce(f32[1000,400]{0,1:T(8,128)S(1)} %select_select_fusion.1), channel_id=1, replica_groups=mesh['dom'=8,'grp'=16] {'grp'}, use_global_device_ids=true, to_apply=%region_7.12 | all-reduce | flops 400000 | bytes 2400000 | tf_op jit(solution)/shard_map/psum | solution.py:51
  181.1 17.3 %gather_fusion.1 = bf16[4096,400]{1,0:T(8,128)(2,1)} fusion(bf16[1024,400]{1,0:T(8,128)(2,1)S(1)} %copy.82, s32[4096]{0:T(1024)S(1)} %fusion.48), kind=kCustom, calls=%fused_computation.2.clone | custom fusion | bytes 6569984 | tf_op jit(solution)/shard_map/jit(_take)/gather | solution.py:83
  198.4 6.0 copy.83
  206.9 8.0 fusion.77
  216.1 7.9 fusion
  224.0 7.6 multiply_convert_fusion.1
  231.6 4.4 fusion.3
  238.1 4.6 all-to-all-start.2
  242.8 21.5 %all-gather = f32[8,1,128]{2,1,0:T(1,128)S(1)} all-gather(f32[1,1,128]{2,1,0:T(1,128)S(1)} %bitcast.173), channel_id=1, replica_groups=mesh['dom'=8,'grp'=16] {'dom'}, dimensions={0}, use_global_device_ids=true | all-gather | bytes 4608 | tf_op jit(solution)/shard_map/all_gather | solution.py:24
  270.0 6.0 copy.87
  276.0 15.2 %scatter_custom_fusion.2 = f32[128,400]{1,0:T(8,128)} fusion(s32[1024]{0:T(1024)} %bitcast.169, pred[1024]{0:T(1024)(128)(4,1)} %compare_and_fusion.4, bf16[]{:T(256)} %constant.29.clone.2, f32[]{:T(128)} %constant.60.clone.1, bf16[4096,400]{1,0:T(8,128)(2,1)} %bitcast.126, s32[1024]{0:T(1024)} %broadcast_clamp_fusion.3), kind=kCustom, calls=%fused_computation.54 | custom fusion | flops 1228800 | bytes 4405248 | tf_op jit(solution)/shard_map/scatter-add | solution.py:106
  295.0 5.0 scatter_custom_fusion.3
  300.1 16.7 %all-to-all-start.3 = ((s32[16,1,256]{2,1,0:T(1,128)}), s32[16,1,256]{2,1,0:T(1,128)}, u32[]{:S(2)}, u32[]{:S(2)}) async-start(s32[16,1,256]{2,1,0:T(1,128)} %bitcast.32), calls=%async_computation.3 | async-start | bytes 32768 | tf_op jit(solution)/shard_map/all_to_all | solution.py:71
  324.4 11.6 %all-gather.11.cloned.1.call-done = f32[1024,400]{1,0:T(8,128)} async-done(((f32[128,400]{1,0:T(8,128)}), f32[1024,400]{1,0:T(8,128)}) %all-gather.11.cloned.1.call-update) | async-done | bytes 1638416 | tf_op jit(solution)/shard_map/all_gather | solution.py:23
  344.6 7.2 fusion.79
  352.4 13.7 %all-gather.13.cloned.1.call-done = f32[1024,400]{1,0:T(8,128)} async-done(((f32[128,400]{1,0:T(8,128)}), f32[1024,400]{1,0:T(8,128)}) %all-gather.13.cloned.1.call-update) | async-done | bytes 1638416 | tf_op jit(solution)/shard_map/all_gather | solution.py:23
  370.1 15.9 %scatter_custom_fusion.4 = bf16[4096,400]{1,0:T(8,128)(2,1)} fusion(s32[1024]{0:T(1024)} %bitcast.164, bf16[]{:T(256)} %constant.84.clone.1, pred[1024]{0:T(1024)(128)(4,1)S(1)} %copy-done.40, bf16[]{:T(256)} %constant.29.clone.2, bf16[128,400]{1,0:T(8,128)(2,1)} %fusion.39, s32[1024]{0:T(1024)S(1)} %copy-done.32), kind=kCustom, calls=%fused_computation.56 | custom fusion | flops 409600 | bytes 3414016 | tf_op jit(solution)/shard_map/scatter | solution.py:61
  385.9 6.1 copy.90
  392.0 6.8 all-to-all-start.4
  403.2 8.5 %copy.92 = f32[4096,400]{1,0:T(8,128)} copy(f32[4096,400]{0,1:T(8,128)} %convert_multiply_fusion.2) | data formatting | bytes 13107200 | tf_op jit(solution)/shard_map/mul | solution.py:110
  411.7 29.3 %scatter_custom_fusion.5 = f32[1024,400]{1,0:T(8,128)S(1)} fusion(s32[4096]{0:T(1024)} %bitcast.161, f32[4096,400]{1,0:T(8,128)} %copy.92, f32[]{:T(128)} %constant.60.clone.1), kind=kCustom, calls=%fused_computation.68 | custom fusion | flops 1638400 | bytes 1638912 | tf_op jit(solution)/shard_map/scatter-add | solution.py:110
  441.0 48.3 %all-reduce.5.cloned.1.call-done = f32[1000,400]{0,1:T(8,128)} async-done(((f32[1000,400]{0,1:T(8,128)}), f32[1000,400]{0,1:T(8,128)}) %all-reduce.5.cloned.1.call-update) | async-done | bytes 1600016 | tf_op jit(solution)/shard_map/psum | solution.py:115
  495.0 8.7 %scatter_fusion = f32[1024,400]{1,0:T(8,128)S(1)} fusion(f32[1024,400]{1,0:T(8,128)S(1)} %scatter_custom_fusion.5, s32[1000]{0:T(1024)S(1)} %bitcast.151, f32[1000,400]{1,0:T(8,128)} %copy.93), kind=kCustom, calls=%fused_computation.22 | custom fusion | flops 400000 | bytes 4804000 | tf_op jit(solution)/shard_map/scatter-add | solution.py:116
  507.1 5.7 gather_fusion.7
  516.2 17.3 %gather_fusion.6 = bf16[4096,400]{1,0:T(8,128)(2,1)} fusion(bf16[1024,400]{1,0:T(8,128)(2,1)S(1)} %get-tuple-element.32, s32[4096]{0:T(1024)S(1)} %copy-done.16), kind=kCustom, calls=%fused_computation.10.clone | custom fusion | bytes 6569984 | tf_op jit(solution)/shard_map/jit(_take)/gather | solution.py:83
  533.5 6.0 copy.95
  539.5 73.8 %all-reduce.9 = bf16[1000,400]{0,1:T(8,128)(2,1)} all-reduce(f32[1000,400]{0,1:T(8,128)S(1)} %select_select_fusion), channel_id=1, replica_groups=mesh['dom'=8,'grp'=16] {'grp'}, use_global_device_ids=true, to_apply=%region_21.28 | all-reduce | flops 400000 | bytes 2400000 | tf_op jit(solution)/shard_map/psum | solution.py:51
  615.7 8.0 fusion.78
  625.0 7.9 fusion.1
  632.9 7.6 multiply_convert_fusion
  646.9 4.5 all-to-all-start.5
  652.2 7.2 fusion.80
  661.8 28.2 %all-gather.1 = f32[8,1,128]{2,1,0:T(1,128)S(1)} all-gather(f32[1,1,128]{2,1,0:T(1,128)} %bitcast.171), channel_id=1, replica_groups=mesh['dom'=8,'grp'=16] {'dom'}, dimensions={0}, use_global_device_ids=true | all-gather | bytes 4608 | tf_op jit(solution)/shard_map/all_gather | solution.py:24
  692.3 8.5 %all-gather.2 = f32[8,1,128]{2,1,0:T(1,128)S(1)} all-gather(f32[1,1,128]{2,1,0:T(1,128)S(1)} %fusion.62), channel_id=1, replica_groups=mesh['dom'=8,'grp'=16] {'dom'}, dimensions={0}, use_global_device_ids=true | all-gather | bytes 4608 | tf_op jit(solution)/shard_map/all_gather | solution.py:24
  702.4 6.0 copy.98
  708.4 15.0 %scatter_custom_fusion.7 = f32[128,400]{1,0:T(8,128)} fusion(s32[1024]{0:T(1024)} %bitcast.165, pred[1024]{0:T(1024)(128)(4,1)S(1)} %copy-done.41, bf16[]{:T(256)} %constant.29.clone.2, f32[]{:T(128)} %constant.60.clone.1, bf16[4096,400]{1,0:T(8,128)(2,1)} %bitcast.125, s32[1024]{0:T(1024)S(1)} %copy-done.31), kind=kCustom, calls=%fused_computation.50 | custom fusion | flops 1228800 | bytes 4405248 | tf_op jit(solution)/shard_map/scatter-add | solution.py:106
  732.1 8.6 %copy.99 = f32[4096,400]{1,0:T(8,128)} copy(f32[4096,400]{0,1:T(8,128)} %convert_multiply_fusion) | data formatting | bytes 13107200 | tf_op jit(solution)/shard_map/mul | solution.py:110
  740.6 29.4 %scatter_custom_fusion.8 = f32[1024,400]{1,0:T(8,128)S(1)} fusion(s32[4096]{0:T(1024)S(1)} %bitcast.162, f32[4096,400]{1,0:T(8,128)} %copy.99, f32[]{:T(128)} %constant.60.clone.1), kind=kCustom, calls=%fused_computation.66 | custom fusion | flops 1638400 | bytes 1638912 | tf_op jit(solution)/shard_map/scatter-add | solution.py:110
  776.1 8.8 %scatter_fusion.1 = f32[1024,400]{1,0:T(8,128)S(1)} fusion(f32[1024,400]{1,0:T(8,128)S(1)} %scatter_custom_fusion.8, s32[1000]{0:T(1024)S(1)} %bitcast.152, f32[1000,400]{1,0:T(8,128)} %copy.100), kind=kCustom, calls=%fused_computation.25 | custom fusion | flops 400000 | bytes 4804000 | tf_op jit(solution)/shard_map/scatter-add | solution.py:116
  791.1 12.7 %all-gather.3 = f32[8,1,128]{2,1,0:T(1,128)S(1)} all-gather(f32[1,1,128]{2,1,0:T(1,128)S(1)} %bitcast.172), channel_id=1, replica_groups=mesh['dom'=8,'grp'=16] {'dom'}, dimensions={0}, use_global_device_ids=true | all-gather | bytes 4608 | tf_op jit(solution)/shard_map/all_gather | solution.py:24
  (232 shorter events, 117.1 us)
Async XLA Ops:
  7.2 32.2 %all-gather.9.cloned.1.call-start = ((), (), s32[]{:S(2)}) async-start(), calls=%async_computation.6 | async-start | bytes 2359296 | tf_op jit(solution)/shard_map/all_gather | solution.py:23
  9.7 28.6 %copy-start.14 = (s32[1,1024,1]{1,2,0:T(1,128)}, s32[1,1024,1]{1,2,0:T(1,128)S(1)}, u32[]{:S(2)}) copy-start(s32[1,1024,1]{1,2,0:T(1,128)S(1)} %get-tuple-element.49) | copy-start | bytes 12292
  19.5 18.8 %copy-start.19 = (s32[1024]{0:T(1024)}, s32[1024]{0:T(1024)S(1)}, u32[]{:S(2)}) copy-start(s32[1024]{0:T(1024)S(1)} %fusion.43) | copy-start | bytes 12292
  27.2 33.8 %all-to-all-start = ((s32[16,1,256]{2,1,0:T(1,128)}), s32[16,1,256]{2,1,0:T(1,128)S(1)}, u32[]{:S(2)}, u32[]{:S(2)}) async-start(s32[16,1,256]{2,1,0:T(1,128)} %bitcast.14), calls=%async_computation | async-start | bytes 32768 | tf_op jit(solution)/shard_map/all_to_all | solution.py:71
  36.9 18.1 %copy-start.43 = (pred[128]{0:T(512)(128)(4,1)}, pred[128]{0:T(512)(128)(4,1)S(1)}, u32[]{:S(2)}) copy-start(pred[128]{0:T(512)(128)(4,1)S(1)} %get-tuple-element.58) | copy-start | bytes 388
  36.9 18.1 %copy-start.44 = (pred[128]{0:T(512)(128)(4,1)}, pred[128]{0:T(512)(128)(4,1)S(1)}, u32[]{:S(2)}) copy-start(pred[128]{0:T(512)(128)(4,1)S(1)} %get-tuple-element.59) | copy-start | bytes 388
  36.9 4.9 copy-start.39
  41.8 19.2 %copy-start.9 = (f32[128,400]{1,0:T(8,128)}, f32[128,400]{1,0:T(8,128)S(1)}, u32[]{:S(2)}) copy-start(f32[128,400]{1,0:T(8,128)S(1)} %gather_fusion) | copy-start | bytes 614404
  61.1 143.3 %all-to-all-start.1 = ((bf16[16,256,400]{1,2,0:T(8,128)(2,1)}), bf16[16,256,400]{1,2,0:T(8,128)(2,1)}, u32[]{:S(2)}, u32[]{:S(2)}) async-start(bf16[16,256,400]{1,2,0:T(8,128)(2,1)} %copy.80), calls=%async_computation.1 | async-start | bytes 6553600 | tf_op jit(solution)/shard_map/all_to_all | solution.py:64
  69.6 7.8 copy-start
  72.5 4.9 copy-start.23
  206.9 8.0 copy-start.5
  224.0 7.6 copy-start.17
  224.0 7.6 copy-start.6
  231.6 4.5 copy-start.7
  238.1 4.7 copy-start.45
  238.1 28.9 %copy-start.27 = (s32[2,1024]{1,0:T(2,128)S(1)}, s32[2,1024]{1,0:T(2,128)}, u32[]{:S(2)}) copy-start(s32[2,1024]{1,0:T(2,128)} %param.25) | copy-start | bytes 24580
  238.1 31.9 %all-to-all-start.2 = ((bf16[16,256,400]{1,2,0:T(8,128)(2,1)}), bf16[16,256,400]{1,2,0:T(8,128)(2,1)}, u32[]{:S(2)}, u32[]{:S(2)}) async-start(bf16[16,256,400]{1,2,0:T(8,128)(2,1)} %bitcast.130), calls=%async_computation.2 | async-start | bytes 6553600 | tf_op jit(solution)/shard_map/all_to_all | solution.py:98
  242.7 93.3 %all-gather.11.cloned.1.call-start = ((), (), s32[]{:S(2)}) async-start(), calls=%async_computation.7 | async-start | bytes 2359296 | tf_op jit(solution)/shard_map/all_gather | solution.py:23
  276.0 17.3 %copy-start.10 = (f32[128,400]{1,0:T(8,128)S(1)}, f32[128,400]{1,0:T(8,128)}, u32[]{:S(2)}) copy-start(f32[128,400]{1,0:T(8,128)} %copy-done.9) | copy-start | bytes 614404
  300.1 40.5 %all-to-all-start.3 = ((s32[16,1,256]{2,1,0:T(1,128)}), s32[16,1,256]{2,1,0:T(1,128)}, u32[]{:S(2)}, u32[]{:S(2)}) async-start(s32[16,1,256]{2,1,0:T(1,128)} %bitcast.32), calls=%async_computation.3 | async-start | bytes 32768 | tf_op jit(solution)/shard_map/all_to_all | solution.py:71
  316.8 49.3 %all-gather.13.cloned.1.call-start = ((), (), s32[]{:S(2)}) async-start(), calls=%async_computation.8 | async-start | bytes 2359296 | tf_op jit(solution)/shard_map/all_gather | solution.py:23
  340.1 149.2 %all-reduce.5.cloned.1.call-start = ((), (), s32[]{:S(2)}) async-start(), calls=%async_computation.9 | async-start | bytes 3276800 | tf_op jit(solution)/shard_map/psum | solution.py:115
  343.3 8.4 %copy-start.13 = (s32[16,1,256]{2,1,0:T(1,128)}, s32[16,1,256]{2,1,0:T(1,128)S(1)}, u32[]{:S(2)}) copy-start(s32[16,1,256]{2,1,0:T(1,128)S(1)} %broadcast_clamp_fusion) | copy-start | bytes 49156
  351.7 16.9 %copy-start.42 = (pred[128]{0:T(512)(128)(4,1)S(1)}, pred[128]{0:T(512)(128)(4,1)}, u32[]{:S(2)}) copy-start(pred[128]{0:T(512)(128)(4,1)} %get-tuple-element.62) | copy-start | bytes 388
  351.7 18.3 %copy-start.32 = (s32[1024]{0:T(1024)S(1)}, s32[1024]{0:T(1024)}, u32[]{:S(2)}) copy-start(s32[1024]{0:T(1024)} %fusion.57) | copy-start | bytes 12292
  351.7 18.3 %copy-start.40 = (pred[1024]{0:T(1024)(128)(4,1)S(1)}, pred[1024]{0:T(1024)(128)(4,1)}, u32[]{:S(2)}) copy-start(pred[1024]{0:T(1024)(128)(4,1)} %compare_and_fusion.3) | copy-start | bytes 3076
  392.0 221.3 %all-to-all-start.4 = ((bf16[16,256,400]{1,2,0:T(8,128)(2,1)}), bf16[16,256,400]{1,2,0:T(8,128)(2,1)}, u32[]{:S(2)}, u32[]{:S(2)}) async-start(bf16[16,256,400]{1,2,0:T(8,128)(2,1)} %copy.90), calls=%async_computation.4 | async-start | bytes 6553600 | tf_op jit(solution)/shard_map/all_to_all | solution.py:64
  403.2 86.2 %copy-start.29 = (pred[1000]{0:T(1024)(128)(4,1)S(1)}, pred[1000]{0:T(1024)(128)(4,1)}, u32[]{:S(2)}) copy-start(pred[1000]{0:T(1024)(128)(4,1)} %copy-done.28) | copy-start | bytes 3004
  441.0 54.0 %copy-start.22 = (s32[1000,1]{0,1:T(1,128)S(1)}, s32[1000,1]{0,1:T(1,128)}, u32[]{:S(2)}) copy-start(s32[1000,1]{0,1:T(1,128)} %get-tuple-element.34) | copy-start | bytes 12004
  495.0 8.9 %copy-start.33 = (f32[1024]{0:T(1024)S(1)}, f32[1024]{0:T(1024)}, u32[]{:S(2)}) copy-start(f32[1024]{0:T(1024)} %param.24) | copy-start | bytes 12292
  615.7 8.0 copy-start.3
  615.7 8.0 copy-start.36
  625.0 7.9 copy-start.26
  625.0 7.9 copy-start.21
  632.9 7.6 copy-start.18
  632.9 7.6 copy-start.4
  646.9 55.5 %all-to-all-start.5 = ((bf16[16,256,400]{1,2,0:T(8,128)(2,1)}), bf16[16,256,400]{1,2,0:T(8,128)(2,1)}, u32[]{:S(2)}, u32[]{:S(2)}) async-start(bf16[16,256,400]{1,2,0:T(8,128)(2,1)} %bitcast.129), calls=%async_computation.5 | async-start | bytes 6553600 | tf_op jit(solution)/shard_map/all_to_all | solution.py:98
  651.4 119.0 %all-reduce.7.cloned.1.call-start = ((), (), s32[]{:S(2)}) async-start(), calls=%async_computation.11 | async-start | bytes 3276800 | tf_op jit(solution)/shard_map/psum | solution.py:115
  652.1 8.5 %copy-start.15 = (s32[1,1024,1]{1,2,0:T(1,128)S(1)}, s32[1,1024,1]{1,2,0:T(1,128)}, u32[]{:S(2)}) copy-start(s32[1,1024,1]{1,2,0:T(1,128)} %copy-done.14) | copy-start | bytes 12292
  652.2 8.5 %copy-start.20 = (s32[1024]{0:T(1024)S(1)}, s32[1024]{0:T(1024)}, u32[]{:S(2)}) copy-start(s32[1024]{0:T(1024)} %copy-done.19) | copy-start | bytes 12292
  659.4 146.1 %all-gather.15.cloned.1.call-start = ((), (), s32[]{:S(2)}) async-start(), calls=%async_computation.10 | async-start | bytes 2359296 | tf_op jit(solution)/shard_map/all_gather | solution.py:23
  702.4 6.0 copy-start.31
  702.4 6.0 copy-start.41
  732.1 38.4 %copy-start.30 = (pred[1000]{0:T(1024)(128)(4,1)S(1)}, pred[1000]{0:T(1024)(128)(4,1)}, u32[]{:S(2)}) copy-start(pred[1000]{0:T(1024)(128)(4,1)} %copy-done.28) | copy-start | bytes 3004
  776.1 9.1 %copy-start.34 = (f32[1024]{0:T(1024)S(1)}, f32[1024]{0:T(1024)}, u32[]{:S(2)}) copy-start(f32[1024]{0:T(1024)} %param.24) | copy-start | bytes 12292
  788.3 19.7 %copy-start.46 = (pred[128]{0:T(512)(128)(4,1)S(1)}, pred[128]{0:T(512)(128)(4,1)}, u32[]{:S(2)}) copy-start(pred[128]{0:T(512)(128)(4,1)} %get-tuple-element.64) | copy-start | bytes 388
  788.3 19.7 %copy-start.47 = (pred[128]{0:T(512)(128)(4,1)S(1)}, pred[128]{0:T(512)(128)(4,1)}, u32[]{:S(2)}) copy-start(pred[128]{0:T(512)(128)(4,1)} %get-tuple-element.65) | copy-start | bytes 388
  (12 other events, 25.3 us)
Sparse Core Ops, SparseCore 0:
  10.3 29.0 all-gather.8
  295.2 40.8 all-gather.10
  340.3 25.7 all-gather.12
  369.8 119.4 all-reduce.4
  659.5 110.9 all-reduce.6
  772.0 26.9 all-gather.14
where the time goes:
time: 828 us; the launch traced here: 816 us
  blocking collectives  242 us (29%)
  other arithmetic  231 us (28%)
  local copies, waits for them, and re-layouts  160 us (19%)
  waiting for transfers between devices  77.6 us (9%)
  starting transfers between devices  47.5 us (6%)
  matrix products  39.2 us (5%)
  between operations  17.8 us (2%)
    psum x2, blocking collectives, train_round(): neg_rows = lax.psum(local_rows, 'grp').astype(jnp.bfloat16)  171 us
    all_gather x4, blocking collectives, relayout(): lax.all_gather(opt_state, 'dom', axis=0, tiled=True)  71 us
    scatter-add x2, other arithmetic, train_round(): tgt_grads = jnp.zeros((tgt_count, emb_width), jnp.float32).at[safe_offset...  58.7 us
    psum x2, waiting for transfers between devices, train_round(): summed = lax.psum(neg_part, 'grp')  48.7 us
    gather x4, local copies, waits for them, and re-layouts, train_round(): target_rows = jnp.take(tgt_bf, safe_offsets, axis=0)  46.6 us
    scatter-add x2, other arithmetic, train_round(): jnp.zeros((src_count, emb_width), jnp.float32).at[sources].add(pair_grad)  30.2 us
    scatter x2, other arithmetic, train_round(): outgoing = jnp.zeros((slot_count, emb_width), jnp.bfloat16).at[slot_place...  28.9 us
    all_gather x4, waiting for transfers between devices, relayout(): lax.all_gather(emb_table, 'dom', axis=0, tiled=True)  26.4 us
  transfers between devices with their start and end apart: 12, of which 6 were waited for; matrix products, arithmetic and copies ran while one was open for 40% of the time, Pallas kernels for 0%

commit v1 on v0

--- a/solution.py
+++ b/solution.py
@@ -112,7 +112,7 @@
     neg_part = lax.dot_general(
         d_neg, incoming, (((0,), (0,)), ((), ())), preferred_element_type=jnp.float32
     )
-    summed = lax.psum(neg_part, "grp")
+    summed = jnp.sum(lax.all_gather(neg_part, "grp"), axis=0)
     tgt_grads = tgt_grads.at[owned_safe].add(jnp.where(is_mine[:, None], summed, 0.0))
     held_table, held_state = adagrad(held_table, held_state, src_grads)
     tgt_table, tgt_state = adagrad(tgt_table, tgt_state, tgt_grads)

time: 828 us -> 1040 us (1.26)
  waiting for transfers between devices: 77.6 us -> 290 us
    all_gather x0 -> x2, waiting for transfers between devices: none -> 228 us  [train_round(): summed = jnp.sum(lax.all_gather(neg_part, 'grp'), axis=0)]
    psum x2 -> x0, waiting for transfers between devices: 48.7 us -> none  [train_round(): summed = lax.psum(neg_part, 'grp')]
    all_gather x4, waiting for transfers between devices: 26.4 us -> 48.6 us  [relayout(): lax.all_gather(emb_table, 'dom', axis=0, tiled=True)]
    reduce_sum x0 -> x2, other arithmetic: none -> 20.9 us  [train_round(): summed = jnp.sum(lax.all_gather(neg_part, 'grp'), axis=0)]
    all_to_all x2, waiting for transfers between devices: 0.01 us -> 11.5 us  [train_round(): lax.all_to_all(outgoing.reshape(group_count, capacity, emb_width), 'grp',...]
  transfers between devices with their start and end apart: 12 -> 12, of which waited for: 6 -> 7; matrix products, arithmetic and copies ran while one was open for 40% -> 22% of each run, Pallas kernels for 0% -> 0%
where the time goes in v1:
time: 1040 us; the launch traced here: 1030 us
  waiting for transfers between devices  290 us (28%)
  blocking collectives  249 us (24%)
  other arithmetic  240 us (23%)
  local copies, waits for them, and re-layouts  153 us (15%)
  matrix products  42.6 us (4%)
  starting transfers between devices  37.6 us (4%)
  between operations  17.8 us (2%)
    all_gather x2, waiting for transfers between devices, train_round(): summed = jnp.sum(lax.all_gather(neg_part, 'grp'), axis=0)  228 us
    psum x2, blocking collectives, train_round(): neg_rows = lax.psum(local_rows, 'grp').astype(jnp.bfloat16)  177 us
    all_gather x4, blocking collectives, relayout(): lax.all_gather(opt_state, 'dom', axis=0, tiled=True)  71.8 us
    scatter-add x2, other arithmetic, train_round(): tgt_grads = jnp.zeros((tgt_count, emb_width), jnp.float32).at[safe_offset...  60.5 us
    all_gather x4, waiting for transfers between devices, relayout(): lax.all_gather(emb_table, 'dom', axis=0, tiled=True)  48.6 us
    gather x4, local copies, waits for them, and re-layouts, train_round(): target_rows = jnp.take(tgt_bf, safe_offsets, axis=0)  46.7 us
    scatter-add x2, other arithmetic, train_round(): jnp.zeros((src_count, emb_width), jnp.float32).at[sources].add(pair_grad)  29.4 us
    scatter x2, other arithmetic, train_round(): outgoing = jnp.zeros((slot_count, emb_width), jnp.bfloat16).at[slot_place...  26.2 us
  transfers between devices with their start and end apart: 12, of which 7 were waited for; matrix products, arithmetic and copies ran while one was open for 22% of the time, Pallas kernels for 0%

profile of v1, /device:TPU:1, one launch (start us, length us, event | category | flops | bytes accessed | tf_op | source)
XLA Modules:
  0.0 1030.0 jit_solution(5021832760488997402)
XLA Ops:
  21.2 4.9 scatter_custom_fusion
  26.1 7.6 all-to-all-start
  41.9 13.0 %scatter_custom_fusion.1 = bf16[4096,400]{1,0:T(8,128)(2,1)} fusion(s32[1024]{0:T(1024)S(1)} %bitcast.172, bf16[]{:T(256)} %constant.84.clone.1, pred[1024]{0:T(1024)(128)(4,1)S(1)} %compare_and_fusion.6, bf16[]{:T(256)} %constant.29.clone.2, bf16[128,400]{1,0:T(8,128)(2,1)S(1)} %fusion.46, s32[1024]{0:T(1024)S(1)} %fusion.64), kind=kCustom, calls=%fused_computation.58 | custom fusion | flops 409600 | bytes 3412996 | tf_op jit(solution)/shard_map/scatter | solution.py:61
  55.0 6.1 copy.72
  61.0 6.6 all-to-all-start.1
  72.6 4.9 gather_fusion.2
  82.2 98.9 %all-reduce.2 = bf16[1000,400]{1,0:T(8,128)(2,1)} all-reduce(f32[1000,400]{1,0:T(8,128)} %select_select_fusion.1), channel_id=1, replica_groups=mesh['dom'=8,'grp'=16] {'grp'}, use_global_device_ids=true, to_apply=%region_7.12 | all-reduce | flops 400000 | bytes 2400000 | tf_op jit(solution)/shard_map/psum | solution.py:51
  181.3 17.3 %gather_fusion.1 = bf16[4096,400]{1,0:T(8,128)(2,1)} fusion(bf16[1024,400]{1,0:T(8,128)(2,1)S(1)} %copy.74, s32[4096]{0:T(1024)S(1)} %fusion.56), kind=kCustom, calls=%fused_computation.2.clone | custom fusion | bytes 6569984 | tf_op jit(solution)/shard_map/jit(_take)/gather | solution.py:83
  198.5 6.0 copy.75
  207.1 8.0 fusion.85
  216.3 7.9 fusion
  224.2 7.6 multiply_convert_fusion.1
  243.0 22.6 %all-gather.2 = f32[8,1,128]{2,1,0:T(1,128)S(1)} all-gather(f32[1,1,128]{2,1,0:T(1,128)S(1)} %bitcast.177), channel_id=1, replica_groups=mesh['dom'=8,'grp'=16] {'dom'}, dimensions={0}, use_global_device_ids=true | all-gather | bytes 4608 | tf_op jit(solution)/shard_map/all_gather | solution.py:24
  269.5 6.0 copy.78
  275.5 14.3 %scatter_custom_fusion.2 = f32[128,400]{1,0:T(8,128)S(1)} fusion(s32[1024]{0:T(1024)S(1)} %bitcast.173, pred[1024]{0:T(1024)(128)(4,1)S(1)} %compare_and_fusion.4, bf16[]{:T(256)} %constant.29.clone.2, f32[]{:T(128)} %constant.60.clone.1, bf16[4096,400]{1,0:T(8,128)(2,1)} %bitcast.130, s32[1024]{0:T(1024)S(1)} %broadcast_clamp_fusion.3), kind=kCustom, calls=%fused_computation.54 | custom fusion | flops 1228800 | bytes 3486726 | tf_op jit(solution)/shard_map/scatter-add | solution.py:106
  292.8 41.5 %all-gather.17.cloned.1.call-done = f32[1024,400]{1,0:T(8,128)} async-done(((f32[128,400]{1,0:T(8,128)}), f32[1024,400]{1,0:T(8,128)}) %all-gather.17.cloned.1.call-update) | async-done | bytes 1638416 | tf_op jit(solution)/shard_map/all_gather | solution.py:23
  337.7 9.0 convolution_bitcast_fusion.1
  346.7 4.9 scatter_custom_fusion.3
  351.6 6.9 all-to-all-start.3
  366.1 13.2 %scatter_custom_fusion.4 = bf16[4096,400]{1,0:T(8,128)(2,1)} fusion(s32[1024]{0:T(1024)S(1)} %bitcast.168, bf16[]{:T(256)} %constant.84.clone.1, pred[1024]{0:T(1024)(128)(4,1)S(1)} %compare_and_fusion.3, bf16[]{:T(256)} %constant.29.clone.2, bf16[128,400]{1,0:T(8,128)(2,1)S(1)} %fusion.47, s32[1024]{0:T(1024)S(1)} %fusion.65), kind=kCustom, calls=%fused_computation.56 | custom fusion | flops 409600 | bytes 3412996 | tf_op jit(solution)/shard_map/scatter | solution.py:61
  379.3 6.2 copy.81
  385.5 7.0 all-to-all-start.4
  393.8 5.5 convert_multiply_fusion.2
  399.3 8.5 copy.83
  407.8 30.2 %scatter_custom_fusion.5 = f32[1024,400]{1,0:T(8,128)} fusion(s32[4096]{0:T(1024)S(1)} %bitcast.163, f32[4096,400]{1,0:T(8,128)} %copy.83, f32[]{:T(128)} %constant.60.clone.1), kind=kCustom, calls=%fused_computation.74 | custom fusion | flops 1638400 | bytes 1638912 | tf_op jit(solution)/shard_map/scatter-add | solution.py:110
  437.9 11.5 %all-to-all-done.4 = bf16[16,256,400]{1,2,0:T(8,128)(2,1)} async-done(((bf16[16,256,400]{1,2,0:T(8,128)(2,1)}), bf16[16,256,400]{1,2,0:T(8,128)(2,1)}, u32[]{:S(2)}, u32[]{:S(2)}) %all-to-all-start.4) | async-done | bytes 3276832 | tf_op jit(solution)/shard_map/all_to_all | solution.py:64
  449.4 5.0 copy.106
  454.5 104.0 %all-gather.23.cloned.1.call-done = f32[16,1000,400]{1,2,0:T(8,128)} async-done(((f32[1,1000,400]{1,2,0:T(8,128)}), f32[16,1000,400]{1,2,0:T(8,128)}) %all-gather.23.cloned.1.call-update) | async-done | bytes 25600016 | tf_op jit(solution)/shard_map/all_gather | solution.py:115
  558.5 11.0 %reduce_sum.120 = f32[1000,400]{0,1:T(8,128)} reduce(f32[16,1000,400]{1,2,0:T(8,128)} %all-gather.23.cloned.1.call-done, f32[]{:T(128)} %constant.60.clone.1), dimensions={0}, to_apply=%region_18.25 | reduce | flops 6000000 | bytes 27200004 | tf_op jit(solution)/shard_map/reduce_sum | solution.py:115
  572.3 11.9 %scatter_custom_fusion.6 = f32[1024,400]{1,0:T(8,128)} fusion(f32[1024,400]{1,0:T(8,128)} %scatter_custom_fusion.5, s32[1000]{0:T(1024)} %bitcast.165, f32[1000,400]{1,0:T(8,128)} %copy.84, f32[]{:T(128)} %constant.60.clone.1, pred[1000]{0:T(1024)(128)(4,1)S(1)} %and_reduce_fusion), kind=kCustom, calls=%fused_computation.64 | custom fusion | flops 800000 | bytes 3687912 | tf_op jit(solution)/shard_map/scatter-add | solution.py:116
  588.3 5.7 gather_fusion.7
  595.7 78.0 %all-reduce.3 = bf16[1000,400]{1,0:T(8,128)(2,1)} all-reduce(f32[1000,400]{1,0:T(8,128)} %select_select_fusion), channel_id=1, replica_groups=mesh['dom'=8,'grp'=16] {'grp'}, use_global_device_ids=true, to_apply=%region_21.28 | all-reduce | flops 400000 | bytes 2400000 | tf_op jit(solution)/shard_map/psum | solution.py:51
  673.7 17.3 %gather_fusion.6 = bf16[4096,400]{1,0:T(8,128)(2,1)} fusion(bf16[1024,400]{1,0:T(8,128)(2,1)S(1)} %get-tuple-element.32, s32[4096]{0:T(1024)S(1)} %fusion.57), kind=kCustom, calls=%fused_computation.10.clone | custom fusion | bytes 6569984 | tf_op jit(solution)/shard_map/jit(_take)/gather | solution.py:83
  690.9 6.2 copy.86
  697.1 9.3 fusion.86
  707.7 7.9 fusion.1
  715.6 7.9 multiply_convert_fusion
  735.4 23.1 %all-gather.4 = f32[8,1,128]{2,1,0:T(1,128)S(1)} all-gather(f32[1,1,128]{2,1,0:T(1,128)} %bitcast.175), channel_id=1, replica_groups=mesh['dom'=8,'grp'=16] {'dom'}, dimensions={0}, use_global_device_ids=true | all-gather | bytes 4608 | tf_op jit(solution)/shard_map/all_gather | solution.py:24
  760.9 8.5 all-gather.5
  771.1 6.0 copy.88
  777.1 15.0 %scatter_custom_fusion.7 = f32[128,400]{1,0:T(8,128)} fusion(s32[1024]{0:T(1024)} %bitcast.169, pred[1024]{0:T(1024)(128)(4,1)S(1)} %copy-done.38, bf16[]{:T(256)} %constant.29.clone.2, f32[]{:T(128)} %constant.60.clone.1, bf16[4096,400]{1,0:T(8,128)(2,1)} %bitcast.129, s32[1024]{0:T(1024)S(1)} %broadcast_clamp_fusion.2), kind=kCustom, calls=%fused_computation.50 | custom fusion | flops 1228800 | bytes 4405248 | tf_op jit(solution)/shard_map/scatter-add | solution.py:106
  795.7 7.3 convolution_bitcast_fusion
  807.3 8.5 copy.89
  815.8 30.3 %scatter_custom_fusion.8 = f32[1024,400]{1,0:T(8,128)} fusion(s32[4096]{0:T(1024)S(1)} %bitcast.164, f32[4096,400]{1,0:T(8,128)} %copy.89, f32[]{:T(128)} %constant.60.clone.1), kind=kCustom, calls=%fused_computation.72 | custom fusion | flops 1638400 | bytes 1638912 | tf_op jit(solution)/shard_map/scatter-add | solution.py:110
  846.1 17.6 %all-gather.6 = f32[8,1,128]{2,1,0:T(1,128)S(1)} all-gather(f32[1,1,128]{2,1,0:T(1,128)S(1)} %bitcast.176), channel_id=1, replica_groups=mesh['dom'=8,'grp'=16] {'dom'}, dimensions={0}, use_global_device_ids=true | all-gather | bytes 4608 | tf_op jit(solution)/shard_map/all_gather | solution.py:24
  868.5 123.5 %all-gather.25.cloned.1.call-done = f32[16,1000,400]{1,2,0:T(8,128)} async-done(((f32[1,1000,400]{1,2,0:T(8,128)}), f32[16,1000,400]{1,2,0:T(8,128)}) %all-gather.25.cloned.1.call-update) | async-done | bytes 25600016 | tf_op jit(solution)/shard_map/all_gather | solution.py:115
  992.1 9.9 reduce_sum.124
  1003.8 12.1 %scatter_custom_fusion.9 = f32[1024,400]{1,0:T(8,128)} fusion(f32[1024,400]{1,0:T(8,128)} %scatter_custom_fusion.8, s32[1000]{0:T(1024)} %bitcast.166, f32[1000,400]{1,0:T(8,128)} %copy.90, f32[]{:T(128)} %constant.60.clone.1, pred[1000]{0:T(1024)(128)(4,1)S(1)} %copy-done.29), kind=kCustom, calls=%fused_computation.62 | custom fusion | flops 800000 | bytes 3687912 | tf_op jit(solution)/shard_map/scatter-add | solution.py:116
  (220 shorter events, 110.3 us)
Async XLA Ops:
  7.2 32.2 %all-gather.15.cloned.1.call-start = ((), (), s32[]{:S(2)}) async-start(), calls=%async_computation.6 | async-start | bytes 2359296 | tf_op jit(solution)/shard_map/all_gather | solution.py:23
  9.7 45.2 %copy-start.17 = (s32[1,1024,1]{1,2,0:T(1,128)}, s32[1,1024,1]{1,2,0:T(1,128)S(1)}, u32[]{:S(2)}) copy-start(s32[1,1024,1]{1,2,0:T(1,128)S(1)} %get-tuple-element.49) | copy-start | bytes 12292
  19.5 35.4 %copy-start.23 = (s32[1024]{0:T(1024)}, s32[1024]{0:T(1024)S(1)}, u32[]{:S(2)}) copy-start(s32[1024]{0:T(1024)S(1)} %fusion.51) | copy-start | bytes 12292
  26.1 35.0 %all-to-all-start = ((s32[16,1,256]{2,1,0:T(1,128)}), s32[16,1,256]{2,1,0:T(1,128)S(1)}, u32[]{:S(2)}, u32[]{:S(2)}) async-start(s32[16,1,256]{2,1,0:T(1,128)} %bitcast.14), calls=%async_computation | async-start | bytes 32768 | tf_op jit(solution)/shard_map/all_to_all | solution.py:71
  61.0 143.5 %all-to-all-start.1 = ((bf16[16,256,400]{1,2,0:T(8,128)(2,1)}), bf16[16,256,400]{1,2,0:T(8,128)(2,1)}, u32[]{:S(2)}, u32[]{:S(2)}) async-start(bf16[16,256,400]{1,2,0:T(8,128)(2,1)} %copy.72), calls=%async_computation.1 | async-start | bytes 6553600 | tf_op jit(solution)/shard_map/all_to_all | solution.py:64
  77.5 494.8 %copy-start.27 = (pred[1000]{0:T(1024)(128)(4,1)}, pred[1000]{0:T(1024)(128)(4,1)S(1)}, u32[]{:S(2)}) copy-start(pred[1000]{0:T(1024)(128)(4,1)S(1)} %and_reduce_fusion) | copy-start | bytes 3004
  77.5 103.6 %copy-start.34 = (pred[1000]{0:T(1024)(128)(4,1)}, pred[1000]{0:T(1024)(128)(4,1)S(1)}, u32[]{:S(2)}) copy-start(pred[1000]{0:T(1024)(128)(4,1)S(1)} %compare_and_fusion.5) | copy-start | bytes 3004
  181.2 23.3 %copy-start.13 = (s32[16,1,256]{2,1,0:T(1,128)}, s32[16,1,256]{2,1,0:T(1,128)S(1)}, u32[]{:S(2)}) copy-start(s32[16,1,256]{2,1,0:T(1,128)S(1)} %broadcast_clamp_fusion.1) | copy-start | bytes 49156
  207.0 8.0 copy-start.1
  207.1 8.0 copy-start.5
  224.2 7.6 copy-start.19
  224.2 7.6 copy-start.6
  238.3 4.7 copy-start.42
  238.3 28.3 %copy-start.26 = (s32[2,1024]{1,0:T(2,128)S(1)}, s32[2,1024]{1,0:T(2,128)}, u32[]{:S(2)}) copy-start(s32[2,1024]{1,0:T(2,128)} %param.25) | copy-start | bytes 24580
  238.3 31.2 %all-to-all-start.2 = ((bf16[16,256,400]{1,2,0:T(8,128)(2,1)}), bf16[16,256,400]{1,2,0:T(8,128)(2,1)}, u32[]{:S(2)}, u32[]{:S(2)}) async-start(bf16[16,256,400]{1,2,0:T(8,128)(2,1)} %bitcast.134), calls=%async_computation.2 | async-start | bytes 6553600 | tf_op jit(solution)/shard_map/all_to_all | solution.py:98
  243.0 91.4 %all-gather.17.cloned.1.call-start = ((), (), s32[]{:S(2)}) async-start(), calls=%async_computation.7 | async-start | bytes 2359296 | tf_op jit(solution)/shard_map/all_gather | solution.py:23
  275.5 16.0 %copy-start.39 = (s32[2,8]{1,0:T(2,128)S(1)}, s32[2,8]{1,0:T(2,128)}, u32[]{:S(2)}) copy-start(s32[2,8]{1,0:T(2,128)} %param.29) | copy-start | bytes 196
  291.4 72.1 %all-gather.19.cloned.1.call-start = ((), (), s32[]{:S(2)}) async-start(), calls=%async_computation.8 | async-start | bytes 2359296 | tf_op jit(solution)/shard_map/all_gather | solution.py:23
  292.8 53.9 %copy-start.36 = (s32[1024]{0:T(1024)}, s32[1024]{0:T(1024)S(1)}, u32[]{:S(2)}) copy-start(s32[1024]{0:T(1024)S(1)} %pad_clamp_fusion.2) | copy-start | bytes 12292
  337.6 220.9 %all-gather.23.cloned.1.call-start = ((), (), s32[]{:S(2)}) async-start(), calls=%async_computation.10 | async-start | bytes 27852800 | tf_op jit(solution)/shard_map/all_gather | solution.py:115
  351.6 33.9 %all-to-all-start.3 = ((s32[16,1,256]{2,1,0:T(1,128)}), s32[16,1,256]{2,1,0:T(1,128)S(1)}, u32[]{:S(2)}, u32[]{:S(2)}) async-start(s32[16,1,256]{2,1,0:T(1,128)} %bitcast.32), calls=%async_computation.3 | async-start | bytes 32768 | tf_op jit(solution)/shard_map/all_to_all | solution.py:71
  359.2 20.0 %copy-start.40 = (pred[128]{0:T(512)(128)(4,1)}, pred[128]{0:T(512)(128)(4,1)S(1)}, u32[]{:S(2)}) copy-start(pred[128]{0:T(512)(128)(4,1)S(1)} %get-tuple-element.62) | copy-start | bytes 388
  359.2 20.0 %copy-start.41 = (pred[128]{0:T(512)(128)(4,1)}, pred[128]{0:T(512)(128)(4,1)S(1)}, u32[]{:S(2)}) copy-start(pred[128]{0:T(512)(128)(4,1)S(1)} %get-tuple-element.63) | copy-start | bytes 388
  359.3 6.7 copy-start.37
  385.5 8.3 copy-start.14
  385.5 8.3 copy-start.20
  385.5 64.0 %all-to-all-start.4 = ((bf16[16,256,400]{1,2,0:T(8,128)(2,1)}), bf16[16,256,400]{1,2,0:T(8,128)(2,1)}, u32[]{:S(2)}, u32[]{:S(2)}) async-start(bf16[16,256,400]{1,2,0:T(8,128)(2,1)} %copy.81), calls=%async_computation.4 | async-start | bytes 6553600 | tf_op jit(solution)/shard_map/all_to_all | solution.py:64
  393.1 6.1 copy-start.15
  572.3 13.9 %copy-start.30 = (f32[1024]{0:T(1024)S(1)}, f32[1024]{0:T(1024)}, u32[]{:S(2)}) copy-start(f32[1024]{0:T(1024)} %param.24) | copy-start | bytes 12292
  588.3 5.7 copy-start.28
  588.3 5.7 copy-start.35
  690.9 6.2 copy-start.2
  697.1 9.3 copy-start.7
  697.1 9.4 copy-start.33
  707.7 7.9 copy-start.25
  715.6 8.0 copy-start.21
  715.6 8.0 copy-start.8
  715.6 8.0 copy-start.12
  730.2 4.7 copy-start.18
  730.2 4.7 copy-start.24
  730.2 40.9 %all-to-all-start.5 = ((bf16[16,256,400]{1,2,0:T(8,128)(2,1)}), bf16[16,256,400]{1,2,0:T(8,128)(2,1)}, u32[]{:S(2)}, u32[]{:S(2)}) async-start(bf16[16,256,400]{1,2,0:T(8,128)(2,1)} %bitcast.133), calls=%async_computation.5 | async-start | bytes 6553600 | tf_op jit(solution)/shard_map/all_to_all | solution.py:98
  734.8 130.3 %all-gather.21.cloned.1.call-start = ((), (), s32[]{:S(2)}) async-start(), calls=%async_computation.9 | async-start | bytes 2359296 | tf_op jit(solution)/shard_map/all_gather | solution.py:23
  771.1 6.0 copy-start.38
  795.7 8.1 copy-start.16
  795.7 8.1 copy-start.22
  795.7 196.4 %all-gather.25.cloned.1.call-start = ((), (), s32[]{:S(2)}) async-start(), calls=%async_computation.11 | async-start | bytes 27852800 | tf_op jit(solution)/shard_map/all_gather | solution.py:115
  1003.8 14.0 %copy-start.31 = (f32[1024]{0:T(1024)S(1)}, f32[1024]{0:T(1024)}, u32[]{:S(2)}) copy-start(f32[1024]{0:T(1024)} %param.24) | copy-start | bytes 12292
  1003.8 14.7 %copy-start = (f32[1024,400]{1,0:T(8,128)S(1)}, f32[1024,400]{1,0:T(8,128)}, u32[]{:S(2)}) copy-start(f32[1024,400]{1,0:T(8,128)} %get-tuple-element.33) | copy-start | bytes 4915204
  (7 other events, 22.5 us)
Sparse Core Ops, SparseCore 0:
  10.3 29.0 all-gather.14
  291.5 42.7 all-gather.16
  337.7 25.7 all-gather.18
  366.1 192.3 all-gather.22
  795.8 34.6 all-gather.20
  833.0 158.9 all-gather.24
